TPU v7x, 32 devices: a whole 2x2x4 slice. The times are simulated.
32 devices in a mesh: date: 2 (over y), trade: 8 (over z, x), path: 2 (over core).
Axes of the slice: x: 2, y: 2, z: 4, core: 2. Of those that a mesh axis runs over, the one named last changes fastest.
Arguments:
- basis_values: bfloat16 [2048, 512], P(('date', 'path')), parts along dimension 0, may hold values from -6 to 6
- coefficients: bfloat16 [2560, 512], P(('date', 'trade')), parts along dimension 0, may hold values from -0.25 to 0.25
- trade_cpty: int32 [1280], P('trade'), may hold values from 0 to 127, as said below
- trade_bucket: int32 [1280], P('trade'), may hold values from 0 to 127
- risk_weights: float32 [128], replicated, may hold values from 0.5 to 2
- correlation: float32 [128, 128], replicated, may hold values from 0 to 1, as said below
- funding_spread: float32 [128], P('trade'), may hold values from 0.5 to 2
Outputs:
- margin: float32 [128, 2048], P('trade', ('date', 'path')), parts along dimension 1
- basis_adjoint: bfloat16 [2048, 512], P(('date', 'path')), parts along dimension 0
There are 2 independent parts, one for each index of `date`. A program takes and returns all parts, laid end to end along the dimension named above; an argument that names none is the same for every part. Nothing has to cross between parts.
Inputs may be any that keep to these rules, and one draw needn't show every extreme that they name: `trade_cpty`: counterparty c belongs to owner block c // 16. Among the trades of one device, at most 40 belong to counterparties of one owner block; in every draw one owner block receives exactly 40 from every device. Counterparties differ in size. `correlation`: symmetric positive definite with unit diagonal; smallest eigenvalue at least 0.01; entries positive.
All inputs are finite; a program needn't handle non-finite values.
Results may differ from a plain program's by a relative error of at most 0.0034.
Values may be sent and summed in bfloat16 or wider, within the bound.
No kernel may reach another device: no remote copies, remote signals or barrier semaphores. Data moves between devices by JAX's collectives and lax.ppermute only.
A program may use at most 64 MiB of HBM per device.

v0:
```python
import jax
import jax.numpy as jnp
from jax import lax
from jax.sharding import PartitionSpec as P


def margin_terms(arrived, got_codes, risk_weights, correlation, funding_spread):
    path_rows = arrived.shape[0]
    cpty_count = funding_spread.shape[0]
    bucket_count = risk_weights.shape[0]
    is_filled = got_codes >= 0
    column_ids = jnp.arange(cpty_count * bucket_count, dtype=jnp.int32)
    hot_table = (got_codes[:, None] == column_ids[None, :]).astype(jnp.bfloat16)
    bucket_sums = jnp.dot(arrived, hot_table, preferred_element_type=jnp.float32)
    weighted = (
        bucket_sums.reshape(path_rows, cpty_count, bucket_count) * risk_weights[None, None, :]
    )
    rho_w = jnp.einsum("pcb,db->pcd", weighted, correlation, precision=lax.Precision.HIGHEST)
    margin_now = jnp.sqrt(jnp.sum(weighted * rho_w, axis=2) + 1e-06)
    sens_bar = (
        funding_spread[None, :, None] * risk_weights[None, None, :] * rho_w / margin_now[:, :, None]
    )
    flat_bar = sens_bar.reshape(path_rows, cpty_count * bucket_count)
    safe_codes = jnp.where(is_filled, got_codes, 0)
    slot_bar = jnp.take(flat_bar, safe_codes, axis=1) * is_filled[None, :].astype(jnp.float32)
    return (margin_now, slot_bar.astype(jnp.bfloat16))


def body(
    basis_values, coefficients, trade_cpty, trade_bucket, risk_weights, correlation, funding_spread
):
    owners = lax.axis_size("trade")
    per_device = coefficients.shape[0]
    capacity = max(2, 2 * per_device // owners)
    slot_total = owners * capacity
    cpty_count = funding_spread.shape[0]
    bucket_count = risk_weights.shape[0]
    path_rows = basis_values.shape[0]
    owner_of = trade_cpty // cpty_count
    trade_code = trade_cpty % cpty_count * bucket_count + trade_bucket
    position = jnp.arange(per_device, dtype=jnp.int32)
    same_owner = owner_of[:, None] == owner_of[None, :]
    earlier = position[None, :] < position[:, None]
    rank_in = jnp.sum((same_owner & earlier).astype(jnp.int32), axis=1)
    slot_index = owner_of * capacity + rank_in
    codes_out = jnp.full((slot_total,), -1, jnp.int32).at[slot_index].set(trade_code)
    got_codes = lax.all_to_all(codes_out, "trade", split_axis=0, concat_axis=0, tiled=True)
    delta_rows = lax.dot_general(
        basis_values, coefficients, (((1,), (1,)), ((), ())), preferred_element_type=jnp.float32
    ).astype(jnp.bfloat16)
    outgoing = jnp.zeros((path_rows, slot_total), jnp.bfloat16).at[:, slot_index].set(delta_rows)
    arrived = lax.all_to_all(outgoing, "trade", split_axis=1, concat_axis=1, tiled=True)
    margin_now, slot_bar = margin_terms(
        arrived, got_codes, risk_weights, correlation, funding_spread
    )
    returned = lax.all_to_all(slot_bar, "trade", split_axis=1, concat_axis=1, tiled=True)
    delta_bar = returned[:, slot_index]
    partial_adj = jnp.dot(delta_bar, coefficients, preferred_element_type=jnp.float32)
    basis_adjoint = lax.psum(partial_adj, "trade").astype(jnp.bfloat16)
    return (margin_now.T, basis_adjoint)


def solution(mesh):
    placed = (
        P(("date", "path"), None),
        P(("date", "trade"), None),
        P("trade"),
        P("trade"),
        P(),
        P(),
        P("trade"),
    )
    return jax.shard_map(
        body,
        mesh=mesh,
        in_specs=placed,
        out_specs=(P("trade", ("date", "path")), P(("date", "path"), None)),
        check_vma=False,
    )
```

profile of v0, /device:TPU:0, one launch (start us, length us, event | category | flops | bytes accessed | tf_op | source)
XLA Modules:
  0.0 130.3 jit_solution(14144373721821639996)
XLA Ops:
  0.6 0.8 fusion.14
  1.4 0.2 convert_reduce_fusion
  1.6 1.1 scatter_custom_fusion.1
  2.7 0.7 all_to_all.25
  3.4 7.3 %all-to-all-start.1 = ((s32[8,40,1]{1,2,0:T(1,128)}), s32[8,40,1]{1,2,0:T(1,128)S(1)}, u32[]{:S(2)}, u32[]{:S(2)}) async-start(s32[8,40,1]{1,2,0:T(1,128)} %all_to_all.25), calls=%async_computation.1 | async-start | bytes 8192 | tf_op jit(solution)/shard_map/all_to_all | solution.py:47
  10.7 1.2 fusion.7
  11.9 1.9 %scatter_custom_fusion = bf16[512,320]{0,1:T(8,128)(2,1)} fusion(s32[160]{0:T(256)S(1)} %compare_select_fusion.4, bf16[160,512]{1,0:T(8,128)(2,1)S(1)} %fusion.7, bf16[]{:T(256)} %constant.45.clone.1), kind=kCustom, calls=%fused_computation.18 | custom fusion | bytes 327682 | tf_op jit(solution)/shard_map/scatter | solution.py:51
  13.8 3.2 %all-to-all-done.1 = s32[8,40,1]{1,2,0:T(1,128)S(1)} async-done(((s32[8,40,1]{1,2,0:T(1,128)}), s32[8,40,1]{1,2,0:T(1,128)S(1)}, u32[]{:S(2)}, u32[]{:S(2)}) %all-to-all-start.1) | async-done | bytes 1312 | tf_op jit(solution)/shard_map/all_to_all | solution.py:47
  17.0 3.4 %all-to-all-start = ((bf16[512,8,40]{0,2,1:T(8,128)(2,1)}), bf16[512,8,40]{0,2,1:T(8,128)(2,1)S(1)}, u32[]{:S(2)}, u32[]{:S(2)}) async-start(bf16[512,8,40]{0,2,1:T(8,128)(2,1)} %bitcast.1), calls=%async_computation | async-start | bytes 655360 | tf_op jit(solution)/shard_map/all_to_all | solution.py:52
  20.5 0.7 broadcast_multiply_fusion
  21.2 0.5 broadcast.164
  21.7 0.7 reduce.7
  22.6 6.9 %all-to-all-done = bf16[512,8,40]{0,2,1:T(8,128)(2,1)S(1)} async-done(((bf16[512,8,40]{0,2,1:T(8,128)(2,1)}), bf16[512,8,40]{0,2,1:T(8,128)(2,1)S(1)}, u32[]{:S(2)}, u32[]{:S(2)}) %all-to-all-start) | async-done | bytes 327712 | tf_op jit(solution)/shard_map/all_to_all | solution.py:52
  29.6 1.4 %fusion.2 = f32[512,16,128]{0,2,1:T(8,128)S(1)} fusion(bf16[512,320,1]{0,1,2:T(8,128)(2,1)S(1)} %bitcast.29, s32[16,128]{1,0:T(8,128)S(1)} %multiply_add_fusion, s32[320]{0:T(512)S(1)} %eq.51), kind=kOutput, calls=%fused_computation.8 | convolution fusion | flops 671744000 | bytes 4531456 | tf_op jit(solution)/shard_map/dot_general | solution.py:14
  31.0 5.5 %multiply_reduce_fusion = (f32[512,16]{0,1:T(8,128)S(1)}, f32[512,16,128]{0,2,1:T(8,128)S(1)}) fusion(f32[512,16,128]{0,2,1:T(8,128)S(1)} %fusion.2, f32[128]{0:T(128)S(1)} %copy-done.3, f32[128,128]{1,0:T(8,128)S(1)} %copy-done.2), kind=kOutput, calls=%fused_computation.5 | convolution fusion | flops 1614798848 | bytes 8487424 | tf_op jit(solution)/shard_map/pcb,db->pcd/dot_general | solution.py:18
  36.4 0.6 add_sqrt_fusion
  37.1 2.4 %multiply_divide_fusion = f32[512,16,128]{0,2,1:T(8,128)} fusion(f32[512,16,128]{0,2,1:T(8,128)S(1)} %get-tuple-element.9, f32[512,16]{0,1:T(8,128)S(1)} %get-tuple-element.2, f32[16,128]{1,0:T(8,128)S(1)} %broadcast_multiply_fusion), kind=kLoop, calls=%fused_computation.4 | loop fusion | flops 2097152 | bytes 8429568 | tf_op jit(solution)/shard_map/div | solution.py:21
  39.5 4.3 %gather_fusion = f32[320,512]{1,0:T(8,128)S(1)} fusion(f32[512,2048]{0,1:T(8,128)} %bitcast.26, s32[1024]{0:T(1024)S(1)} %pad_clamp_fusion.1), kind=kCustom, calls=%fused_computation | custom fusion | bytes 1312000 | tf_op jit(solution)/shard_map/jit(_take)/gather | solution.py:25
  43.8 0.9 multiply_convert_fusion
  44.7 3.6 %all-to-all-start.2 = ((bf16[512,8,40]{0,2,1:T(8,128)(2,1)}), bf16[512,8,40]{0,2,1:T(8,128)(2,1)S(1)}, u32[]{:S(2)}, u32[]{:S(2)}) async-start(bf16[512,8,40]{0,2,1:T(8,128)(2,1)} %multiply_convert_fusion), calls=%async_computation.2 | async-start | bytes 655360 | tf_op jit(solution)/shard_map/all_to_all | solution.py:56
  48.3 9.6 %all-to-all-done.2 = bf16[512,8,40]{0,2,1:T(8,128)(2,1)S(1)} async-done(((bf16[512,8,40]{0,2,1:T(8,128)(2,1)}), bf16[512,8,40]{0,2,1:T(8,128)(2,1)S(1)}, u32[]{:S(2)}, u32[]{:S(2)}) %all-to-all-start.2) | async-done | bytes 327712 | tf_op jit(solution)/shard_map/all_to_all | solution.py:56
  57.9 0.9 gather_fusion.1
  58.8 0.3 fusion.18
  59.2 71.2 %all-reduce.1 = bf16[512,512]{1,0:T(8,128)(2,1)} all-reduce(f32[512,512]{1,0:T(8,128)S(1)} %fusion.18), channel_id=1, replica_groups=mesh['date'=2,'trade'=8,'path'=2] {'trade'}, use_global_device_ids=true, to_apply=%region_4.5 | all-reduce | flops 262144 | bytes 1572864 | tf_op jit(solution)/shard_map/psum | solution.py:59
  (16 shorter events, 0.2 us)
Async XLA Ops:
  0.6 10.0 %copy-start = (bf16[512,512]{1,0:T(8,128)(2,1)S(1)}, bf16[512,512]{1,0:T(8,128)(2,1)}, u32[]{:S(2)}) copy-start(bf16[512,512]{1,0:T(8,128)(2,1)} %param.7) | copy-start | bytes 1572868
  3.4 13.6 %all-to-all-start.1 = ((s32[8,40,1]{1,2,0:T(1,128)}), s32[8,40,1]{1,2,0:T(1,128)S(1)}, u32[]{:S(2)}, u32[]{:S(2)}) async-start(s32[8,40,1]{1,2,0:T(1,128)} %all_to_all.25), calls=%async_computation.1 | async-start | bytes 8192 | tf_op jit(solution)/shard_map/all_to_all | solution.py:47
  11.9 19.0 %copy-start.2 = (f32[128,128]{1,0:T(8,128)S(1)}, f32[128,128]{1,0:T(8,128)}, u32[]{:S(2)}) copy-start(f32[128,128]{1,0:T(8,128)} %param.12) | copy-start | bytes 196612
  11.9 19.0 %copy-start.3 = (f32[128]{0:T(128)S(1)}, f32[128]{0:T(128)}, u32[]{:S(2)}) copy-start(f32[128]{0:T(128)} %param.11) | copy-start | bytes 1540
  17.0 12.5 %all-to-all-start = ((bf16[512,8,40]{0,2,1:T(8,128)(2,1)}), bf16[512,8,40]{0,2,1:T(8,128)(2,1)S(1)}, u32[]{:S(2)}, u32[]{:S(2)}) async-start(bf16[512,8,40]{0,2,1:T(8,128)(2,1)} %bitcast.1), calls=%async_computation | async-start | bytes 655360 | tf_op jit(solution)/shard_map/all_to_all | solution.py:52
  39.5 19.3 %copy-start.1 = (bf16[160,512]{1,0:T(8,128)(2,1)S(1)}, bf16[160,512]{1,0:T(8,128)(2,1)}, u32[]{:S(2)}) copy-start(bf16[160,512]{1,0:T(8,128)(2,1)} %param.8) | copy-start | bytes 491524
  44.7 13.2 %all-to-all-start.2 = ((bf16[512,8,40]{0,2,1:T(8,128)(2,1)}), bf16[512,8,40]{0,2,1:T(8,128)(2,1)S(1)}, u32[]{:S(2)}, u32[]{:S(2)}) async-start(bf16[512,8,40]{0,2,1:T(8,128)(2,1)} %multiply_convert_fusion), calls=%async_computation.2 | async-start | bytes 655360 | tf_op jit(solution)/shard_map/all_to_all | solution.py:56
where the time goes:
time: 131 us; the launch traced here: 130 us
  blocking collectives  71.2 us (54%)
  waiting for transfers between devices  19.8 us (15%)
  starting transfers between devices  14.3 us (11%)
  local copies, waits for them, and re-layouts  9.56 us (7%)
  matrix products  8.42 us (6%)
  other arithmetic  6.37 us (5%)
    psum x1, blocking collectives, body(): basis_adjoint = lax.psum(partial_adj, 'trade').astype(jnp.bfloat16)  71.2 us
    all_to_all x1, waiting for transfers between devices, body(): lax.all_to_all(slot_bar, 'trade', split_axis=1, concat_axis=1, tiled=True)  9.6 us
    all_to_all x1, starting transfers between devices, body(): lax.all_to_all(codes_out, 'trade', split_axis=0, concat_axis=0, tiled=True)  7.25 us
    all_to_all x1, waiting for transfers between devices, body(): lax.all_to_all(outgoing, 'trade', split_axis=1, concat_axis=1, tiled=True)  6.93 us
    dot_general x1, matrix products, margin_terms(): jnp.einsum('pcb,db->pcd', weighted, correlation, precision=lax.Precision....  5.47 us
    gather x1, local copies, waits for them, and re-layouts, margin_terms(): jnp.take(flat_bar, safe_codes, axis=1)  4.27 us
    all_to_all x1, starting transfers between devices, body(): lax.all_to_all(slot_bar, 'trade', split_axis=1, concat_axis=1, tiled=True)  3.6 us
    all_to_all x1, starting transfers between devices, body(): lax.all_to_all(outgoing, 'trade', split_axis=1, concat_axis=1, tiled=True)  3.43 us
  transfers between devices with their start and end apart: 3, of which 3 were waited for; matrix products, arithmetic and copies ran while one was open for 4% of the time, Pallas kernels for 0%

commit v1 on v0

--- a/solution.py
+++ b/solution.py
@@ -49,7 +49,31 @@
         basis_values, coefficients, (((1,), (1,)), ((), ())), preferred_element_type=jnp.float32
     ).astype(jnp.bfloat16)
     outgoing = jnp.zeros((path_rows, slot_total), jnp.bfloat16).at[:, slot_index].set(delta_rows)
-    arrived = lax.all_to_all(outgoing, "trade", split_axis=1, concat_axis=1, tiled=True)
+
+    def compute_corner(array_here):
+        device_axis = "trade"
+        part_next = lax.axis_size(device_axis)
+        built = lax.axis_index(device_axis)
+        e_now, all_rows = (part_next, built)
+        right_arr = list(array_here.shape)
+        h_now = array_here.shape[1] // e_now
+        right_arr[1] = h_now
+        answer = right_arr[1]
+        right_arr[1] = answer * e_now
+        met_up = jnp.zeros(right_arr, array_here.dtype)
+        for dev_i in range(e_now):
+            block_now = lax.dynamic_slice_in_dim(
+                array_here, (all_rows ^ dev_i) * h_now, h_now, axis=1
+            )
+            if dev_i:
+                prior = tuple(((it, it ^ dev_i) for it in range(e_now)))
+                block_now = lax.ppermute(block_now, device_axis, prior)
+            met_up = lax.dynamic_update_slice_in_dim(
+                met_up, block_now, (all_rows ^ dev_i) * answer, axis=1
+            )
+        return met_up
+
+    arrived = compute_corner(outgoing)
     margin_now, slot_bar = margin_terms(
         arrived, got_codes, risk_weights, correlation, funding_spread
     )

time: 131 us -> 135 us (1.031)
  starting transfers between devices: 14.3 us -> 22.2 us
  waiting for transfers between devices: 19.8 us -> 17.7 us
    ppermute x0 -> x7, starting transfers between devices: none -> 12.8 us  [compute_corner(): block_now = lax.ppermute(block_now, device_axis, prior)]
    all_to_all x1 -> x0, waiting for transfers between devices: 6.93 us -> none  [body(): lax.all_to_all(outgoing, 'trade', split_axis=1, concat_axis=1, tiled=True)]
    all_to_all x1 -> x0, starting transfers between devices: 3.43 us -> none  [body(): lax.all_to_all(outgoing, 'trade', split_axis=1, concat_axis=1, tiled=True)]
    ppermute x0 -> x7, waiting for transfers between devices: none -> 3.37 us  [compute_corner(): block_now = lax.ppermute(block_now, device_axis, prior)]
    all_to_all x1, waiting for transfers between devices: 3.23 us -> 5.65 us  [body(): lax.all_to_all(codes_out, 'trade', split_axis=0, concat_axis=0, tiled=True)]
    all_to_all x1, starting transfers between devices: 7.25 us -> 4.88 us  [body(): lax.all_to_all(codes_out, 'trade', split_axis=0, concat_axis=0, tiled=True)]
    dot_general x1 -> x0, matrix products: 1.37 us -> none  [margin_terms(): jnp.dot(arrived, hot_table, preferred_element_type=jnp.float32)]
    reshape x0 -> x1, matrix products: none -> 1.37 us  [margin_terms(): bucket_sums.reshape(path_rows, cpty_count, bucket_count)]
  transfers between devices with their start and end apart: 3 -> 9, of which waited for: 3 -> 4; matrix products, arithmetic and copies ran while one was open for 4% -> 2% of each run, Pallas kernels for 0% -> 0%
where the time goes in v1:
time: 135 us
  blocking collectives  70.4 us (52%)
  starting transfers between devices  22.2 us (16%)
  waiting for transfers between devices  17.7 us (13%)
  local copies, waits for them, and re-layouts  9.13 us (7%)
  matrix products  8.42 us (6%)
  other arithmetic  6.36 us (5%)
    psum x1, blocking collectives, body(): basis_adjoint = lax.psum(partial_adj, 'trade').astype(jnp.bfloat16)  70.4 us
    ppermute x7, starting transfers between devices, compute_corner(): block_now = lax.ppermute(block_now, device_axis, prior)  12.8 us
    all_to_all x1, waiting for transfers between devices, body(): lax.all_to_all(slot_bar, 'trade', split_axis=1, concat_axis=1, tiled=True)  8.65 us
    all_to_all x1, waiting for transfers between devices, body(): lax.all_to_all(codes_out, 'trade', split_axis=0, concat_axis=0, tiled=True)  5.65 us
    dot_general x1, matrix products, margin_terms(): jnp.einsum('pcb,db->pcd', weighted, correlation, precision=lax.Precision....  5.48 us
    all_to_all x1, starting transfers between devices, body(): lax.all_to_all(codes_out, 'trade', split_axis=0, concat_axis=0, tiled=True)  4.88 us
    all_to_all x1, starting transfers between devices, body(): lax.all_to_all(slot_bar, 'trade', split_axis=1, concat_axis=1, tiled=True)  4.54 us
    gather x1, local copies, waits for them, and re-layouts, margin_terms(): jnp.take(flat_bar, safe_codes, axis=1)  4.27 us
  transfers between devices with their start and end apart: 9, of which 4 were waited for; matrix products, arithmetic and copies ran while one was open for 2% of the time, Pallas kernels for 0%

profile of v1, /device:TPU:0, one launch (start us, length us, event | category | flops | bytes accessed | tf_op | source)
XLA Modules:
  0.0 135.1 jit_solution(14995912710386384085)
XLA Ops:
  0.7 0.8 fusion.12
  1.7 1.2 fusion.5
  3.0 1.3 scatter_custom_fusion
  4.4 3.0 %collective-permute-start = (bf16[512,40]{0,1:T(8,128)(2,1)S(1)}, bf16[512,40]{0,1:T(8,128)(2,1)S(1)}, u32[]{:S(2)}, u32[]{:S(2)}) collective-permute-start(bf16[512,40]{0,1:T(8,128)(2,1)S(1)} %get-tuple-element.8), channel_id=1, source_target_pairs={{0,2},{2,0},{4,6},{6,4},{8,10},{10,8},{12,14},{14,12},{1,3},{3,1},... | collective-permute-start | bytes 122888 | tf_op jit(solution)/shard_map/ppermute | solution.py:70
  7.4 1.6 %collective-permute-start.1 = (bf16[512,40]{0,1:T(8,128)(2,1)S(1)}, bf16[512,40]{0,1:T(8,128)(2,1)S(1)}, u32[]{:S(2)}, u32[]{:S(2)}) collective-permute-start(bf16[512,40]{0,1:T(8,128)(2,1)S(1)} %get-tuple-element.7), channel_id=1, source_target_pairs={{0,4},{2,6},{4,0},{6,2},{8,12},{10,14},{12,8},{14,10},{1,5},{3,7},... | collective-permute-start | bytes 122888 | tf_op jit(solution)/shard_map/ppermute | solution.py:70
  9.0 3.0 %collective-permute-start.3 = (bf16[512,40]{0,1:T(8,128)(2,1)S(1)}, bf16[512,40]{0,1:T(8,128)(2,1)S(1)}, u32[]{:S(2)}, u32[]{:S(2)}) collective-permute-start(bf16[512,40]{0,1:T(8,128)(2,1)S(1)} %get-tuple-element.5), channel_id=1, source_target_pairs={{0,8},{2,10},{4,12},{6,14},{8,0},{10,2},{12,4},{14,6},{1,9},{3,11}... | collective-permute-start | bytes 122888 | tf_op jit(solution)/shard_map/ppermute | solution.py:70
  12.0 1.3 collective-permute-start.4
  13.2 1.1 scatter_custom_fusion.1
  14.3 0.7 all_to_all.14
  15.0 4.9 %all-to-all-start = ((s32[8,40,1]{1,2,0:T(1,128)}), s32[8,40,1]{1,2,0:T(1,128)S(1)}, u32[]{:S(2)}, u32[]{:S(2)}) async-start(s32[8,40,1]{1,2,0:T(1,128)} %all_to_all.14), calls=%async_computation | async-start | bytes 8192 | tf_op jit(solution)/shard_map/all_to_all | solution.py:47
  19.9 0.7 broadcast_multiply_fusion
  20.6 5.6 %all-to-all-done = s32[8,40,1]{1,2,0:T(1,128)S(1)} async-done(((s32[8,40,1]{1,2,0:T(1,128)}), s32[8,40,1]{1,2,0:T(1,128)S(1)}, u32[]{:S(2)}, u32[]{:S(2)}) %all-to-all-start) | async-done | bytes 1312 | tf_op jit(solution)/shard_map/all_to_all | solution.py:47
  28.3 3.3 %collective-permute-start.6 = (bf16[512,40]{0,1:T(8,128)(2,1)S(1)}, bf16[512,40]{0,1:T(8,128)(2,1)S(1)}, u32[]{:S(2)}, u32[]{:S(2)}) collective-permute-start(bf16[512,40]{0,1:T(8,128)(2,1)S(1)} %get-tuple-element.2), channel_id=1, source_target_pairs={{0,14},{2,12},{4,10},{6,8},{8,6},{10,4},{12,2},{14,0},{1,15},{3,13... | collective-permute-start | bytes 122888 | tf_op jit(solution)/shard_map/ppermute | solution.py:70
  31.7 1.8 %collective-permute-done.5 = bf16[512,40]{0,1:T(8,128)(2,1)S(1)} collective-permute-done((bf16[512,40]{0,1:T(8,128)(2,1)S(1)}, bf16[512,40]{0,1:T(8,128)(2,1)S(1)}, u32[]{:S(2)}, u32[]{:S(2)}) %collective-permute-start.5) | collective-permute-done | bytes 40992 | tf_op jit(solution)/shard_map/ppermute | solution.py:70
  33.5 1.5 %collective-permute-done.6 = bf16[512,40]{0,1:T(8,128)(2,1)S(1)} collective-permute-done((bf16[512,40]{0,1:T(8,128)(2,1)S(1)}, bf16[512,40]{0,1:T(8,128)(2,1)S(1)}, u32[]{:S(2)}, u32[]{:S(2)}) %collective-permute-start.6) | collective-permute-done | bytes 40992 | tf_op jit(solution)/shard_map/ppermute | solution.py:70
  35.1 1.4 %fusion.2 = f32[512,2048]{0,1:T(8,128)S(1)} fusion(bf16[512,320]{0,1:T(8,128)(2,1)S(1)} %constant_dynamic-update-slice_fusion, s32[320]{0:T(512)S(1)} %eq.35), kind=kOutput, calls=%fused_computation.9 | convolution fusion | flops 671744000 | bytes 4523264 | tf_op jit(solution)/shard_map/reshape | solution.py:16
  36.5 5.5 %multiply_reduce_fusion = (f32[512,16]{0,1:T(8,128)S(1)}, f32[512,16,128]{0,2,1:T(8,128)S(1)}) fusion(f32[128]{0:T(128)S(1)} %copy-done.3, f32[512,2048]{0,1:T(8,128)S(1)} %fusion.2, f32[128,128]{1,0:T(8,128)S(1)} %copy-done.2, f32[512,16,128]{0,2,1:T(8,128)S(1)} %bitcast.24), kind=kOutput, calls=%fused_computation.5 | convolution fusion | flops 1614798848 | bytes 12681728 | tf_op jit(solution)/shard_map/pcb,db->pcd/dot_general | solution.py:18
  42.6 2.5 %multiply_divide_fusion = f32[512,16,128]{0,2,1:T(8,128)} fusion(f32[512,16,128]{0,2,1:T(8,128)S(1)} %get-tuple-element.17, f32[512,16]{0,1:T(8,128)S(1)} %get-tuple-element.10, f32[16,128]{1,0:T(8,128)S(1)} %broadcast_multiply_fusion), kind=kLoop, calls=%fused_computation.4 | loop fusion | flops 2097152 | bytes 8429568 | tf_op jit(solution)/shard_map/div | solution.py:21
  45.0 4.3 %gather_fusion = f32[320,512]{1,0:T(8,128)S(1)} fusion(f32[512,2048]{0,1:T(8,128)} %bitcast.25, s32[1024]{0:T(1024)S(1)} %pad_clamp_fusion.1), kind=kCustom, calls=%fused_computation | custom fusion | bytes 1312000 | tf_op jit(solution)/shard_map/jit(_take)/gather | solution.py:25
  49.3 0.9 multiply_convert_fusion
  50.2 4.5 %all-to-all-start.1 = ((bf16[512,8,40]{0,2,1:T(8,128)(2,1)}), bf16[512,8,40]{0,2,1:T(8,128)(2,1)S(1)}, u32[]{:S(2)}, u32[]{:S(2)}) async-start(bf16[512,8,40]{0,2,1:T(8,128)(2,1)} %multiply_convert_fusion), calls=%async_computation.1 | async-start | bytes 655360 | tf_op jit(solution)/shard_map/all_to_all | solution.py:80
  54.7 8.7 %all-to-all-done.1 = bf16[512,8,40]{0,2,1:T(8,128)(2,1)S(1)} async-done(((bf16[512,8,40]{0,2,1:T(8,128)(2,1)}), bf16[512,8,40]{0,2,1:T(8,128)(2,1)S(1)}, u32[]{:S(2)}, u32[]{:S(2)}) %all-to-all-start.1) | async-done | bytes 327712 | tf_op jit(solution)/shard_map/all_to_all | solution.py:80
  63.4 0.9 gather_fusion.1
  64.7 70.4 %all-reduce.1 = bf16[512,512]{1,0:T(8,128)(2,1)} all-reduce(f32[512,512]{1,0:T(8,128)S(1)} %fusion.16), channel_id=1, replica_groups=mesh['date'=2,'trade'=8,'path'=2] {'trade'}, use_global_device_ids=true, to_apply=%region_4.5 | all-reduce | flops 262144 | bytes 1572864 | tf_op jit(solution)/shard_map/psum | solution.py:83
  (36 shorter events, 3.4 us)
Async XLA Ops:
  0.6 1.1 copy-start
  4.3 32.2 %copy-start.2 = (f32[128,128]{1,0:T(8,128)S(1)}, f32[128,128]{1,0:T(8,128)}, u32[]{:S(2)}) copy-start(f32[128,128]{1,0:T(8,128)} %param.12) | copy-start | bytes 196612
  4.3 32.2 %copy-start.3 = (f32[128]{0:T(128)S(1)}, f32[128]{0:T(128)}, u32[]{:S(2)}) copy-start(f32[128]{0:T(128)} %param.11) | copy-start | bytes 1540
  4.4 23.3 %collective-permute-start = (bf16[512,40]{0,1:T(8,128)(2,1)S(1)}, bf16[512,40]{0,1:T(8,128)(2,1)S(1)}, u32[]{:S(2)}, u32[]{:S(2)}) collective-permute-start(bf16[512,40]{0,1:T(8,128)(2,1)S(1)} %get-tuple-element.8), channel_id=1, source_target_pairs={{0,2},{2,0},{4,6},{6,4},{8,10},{10,8},{12,14},{14,12},{1,3},{3,1},... | collective-permute-start | bytes 122888 | tf_op jit(solution)/shard_map/ppermute | solution.py:70
  7.4 20.9 %collective-permute-start.1 = (bf16[512,40]{0,1:T(8,128)(2,1)S(1)}, bf16[512,40]{0,1:T(8,128)(2,1)S(1)}, u32[]{:S(2)}, u32[]{:S(2)}) collective-permute-start(bf16[512,40]{0,1:T(8,128)(2,1)S(1)} %get-tuple-element.7), channel_id=1, source_target_pairs={{0,4},{2,6},{4,0},{6,2},{8,12},{10,14},{12,8},{14,10},{1,5},{3,7},... | collective-permute-start | bytes 122888 | tf_op jit(solution)/shard_map/ppermute | solution.py:70
  9.0 22.7 %collective-permute-start.2 = (bf16[512,40]{0,1:T(8,128)(2,1)S(1)}, bf16[512,40]{0,1:T(8,128)(2,1)S(1)}, u32[]{:S(2)}, u32[]{:S(2)}) collective-permute-start(bf16[512,40]{0,1:T(8,128)(2,1)S(1)} %get-tuple-element.6), channel_id=1, source_target_pairs={{0,6},{2,4},{4,2},{6,0},{8,14},{10,12},{12,10},{14,8},{1,7},{3,5},... | collective-permute-start | bytes 122888 | tf_op jit(solution)/shard_map/ppermute | solution.py:70
  9.0 22.7 %collective-permute-start.3 = (bf16[512,40]{0,1:T(8,128)(2,1)S(1)}, bf16[512,40]{0,1:T(8,128)(2,1)S(1)}, u32[]{:S(2)}, u32[]{:S(2)}) collective-permute-start(bf16[512,40]{0,1:T(8,128)(2,1)S(1)} %get-tuple-element.5), channel_id=1, source_target_pairs={{0,8},{2,10},{4,12},{6,14},{8,0},{10,2},{12,4},{14,6},{1,9},{3,11}... | collective-permute-start | bytes 122888 | tf_op jit(solution)/shard_map/ppermute | solution.py:70
  12.0 19.7 %collective-permute-start.4 = (bf16[512,40]{0,1:T(8,128)(2,1)S(1)}, bf16[512,40]{0,1:T(8,128)(2,1)S(1)}, u32[]{:S(2)}, u32[]{:S(2)}) collective-permute-start(bf16[512,40]{0,1:T(8,128)(2,1)S(1)} %get-tuple-element.4), channel_id=1, source_target_pairs={{0,10},{2,8},{4,14},{6,12},{8,2},{10,0},{12,6},{14,4},{1,11},{3,9}... | collective-permute-start | bytes 122888 | tf_op jit(solution)/shard_map/ppermute | solution.py:70
  15.0 11.3 %all-to-all-start = ((s32[8,40,1]{1,2,0:T(1,128)}), s32[8,40,1]{1,2,0:T(1,128)S(1)}, u32[]{:S(2)}, u32[]{:S(2)}) async-start(s32[8,40,1]{1,2,0:T(1,128)} %all_to_all.14), calls=%async_computation | async-start | bytes 8192 | tf_op jit(solution)/shard_map/all_to_all | solution.py:47
  27.7 5.9 %collective-permute-start.5 = (bf16[512,40]{0,1:T(8,128)(2,1)S(1)}, bf16[512,40]{0,1:T(8,128)(2,1)S(1)}, u32[]{:S(2)}, u32[]{:S(2)}) collective-permute-start(bf16[512,40]{0,1:T(8,128)(2,1)S(1)} %get-tuple-element.3), channel_id=1, source_target_pairs={{0,12},{2,14},{4,8},{6,10},{8,4},{10,6},{12,0},{14,2},{1,13},{3,15... | collective-permute-start | bytes 122888 | tf_op jit(solution)/shard_map/ppermute | solution.py:70
  28.3 6.8 %collective-permute-start.6 = (bf16[512,40]{0,1:T(8,128)(2,1)S(1)}, bf16[512,40]{0,1:T(8,128)(2,1)S(1)}, u32[]{:S(2)}, u32[]{:S(2)}) collective-permute-start(bf16[512,40]{0,1:T(8,128)(2,1)S(1)} %get-tuple-element.2), channel_id=1, source_target_pairs={{0,14},{2,12},{4,10},{6,8},{8,6},{10,4},{12,2},{14,0},{1,15},{3,13... | collective-permute-start | bytes 122888 | tf_op jit(solution)/shard_map/ppermute | solution.py:70
  45.0 19.3 %copy-start.1 = (bf16[160,512]{1,0:T(8,128)(2,1)S(1)}, bf16[160,512]{1,0:T(8,128)(2,1)}, u32[]{:S(2)}) copy-start(bf16[160,512]{1,0:T(8,128)(2,1)} %param.8) | copy-start | bytes 491524
  50.2 13.2 %all-to-all-start.1 = ((bf16[512,8,40]{0,2,1:T(8,128)(2,1)}), bf16[512,8,40]{0,2,1:T(8,128)(2,1)S(1)}, u32[]{:S(2)}, u32[]{:S(2)}) async-start(bf16[512,8,40]{0,2,1:T(8,128)(2,1)} %multiply_convert_fusion), calls=%async_computation.1 | async-start | bytes 655360 | tf_op jit(solution)/shard_map/all_to_all | solution.py:80
